TPU v7x, 512 devices: a whole 4x8x8 slice. The times are simulated.
512 devices in a mesh: pipe: 8 (over y_hi, core), ctx: 16 (over z, y_lo), dp: 4 (over x).
Axes of the slice: x: 4, y: 8 (y_hi: 4, y_lo: 2; y = y_hi * 2 + y_lo), z: 8, core: 2. Of those that a mesh axis runs over, the one named last changes fastest.
Arguments:
- state: bfloat16 [8, 4, 2048, 1024], P('pipe', 'dp', 'ctx'), may hold values from -36 to 36
- weights: bfloat16 [2, 8, 1024, 256], P(None, 'pipe'), may hold values from -0.1875 to 0.1875
- out_grad: bfloat16 [2, 8, 4, 2048, 1024], P(None, 'pipe', 'dp', 'ctx'), may hold values from -0.59765625 to 0.59765625
- start_span: int32 [8, 4], P(None, 'dp'), may hold values from 0 to 1
- block_order: int32 [32], replicated, may hold values from 0 to 31, each once
Outputs:
- state_out: bfloat16 [8, 4, 2048, 1024], P('pipe', 'dp', 'ctx')
- weight_grads: float32 [2, 8, 1024, 256], P(None, 'pipe')
All inputs are finite; a program needn't handle non-finite values.
Results may differ from a plain program's by a relative error of at most 0.012.
Values may be sent and summed in bfloat16 or wider, within the bound.
No kernel may reach another device: no remote copies, remote signals or barrier semaphores. Data moves between devices by JAX's collectives and lax.ppermute only.
A program may use at most 64 MiB of HBM per device.

v0:
```python
import math
import jax
import jax.numpy as jnp
from jax import lax
from jax.sharding import PartitionSpec as P

EPS = 1e-05


def from_behind(block, axis, distance):
    devices = range(lax.axis_size(axis))
    route = [((i - distance) % len(devices), i) for i in devices]
    return lax.ppermute(block, axis, route)


def rms_scale(values):
    return lax.rsqrt(jnp.mean(values * values, axis=-1, keepdims=True) + EPS)


def token_positions(block_order, seq_total):
    half_count = block_order.shape[0]
    half_len = seq_total // half_count
    row_ids = jnp.arange(seq_total, dtype=jnp.int32)
    selected = (row_ids // half_len)[:, None] == jnp.arange(half_count, dtype=jnp.int32)[None, :]
    block_ids = jnp.sum(jnp.where(selected, block_order[None, :], 0), axis=1)
    return block_ids * half_len + row_ids % half_len


def shards(state, weights, out_grad, start_span, block_order):
    tok_rows = state.shape[2]
    feat_width = state.shape[3]
    head_dim = weights.shape[3] // 2
    head_count = feat_width // head_dim
    group_size = math.gcd(head_count, 4)
    group_count = head_count // group_size
    span_count = weights.shape[0]
    section_count = lax.axis_size("pipe")
    seq_total = tok_rows * lax.axis_size("ctx")
    score_scale = 1.0 / math.sqrt(head_dim)
    all_positions = token_positions(block_order, seq_total)
    own_positions = lax.dynamic_slice_in_dim(
        all_positions, lax.axis_index("ctx") * tok_rows, tok_rows
    )
    causal = all_positions[None, :] <= own_positions[:, None]
    section_index = lax.axis_index("pipe")
    carried = state[0, 0]
    start_column = start_span[:, 0]
    weight_grads = jnp.zeros((span_count, feat_width, 2 * head_dim), jnp.float32)
    for tick_index in range(out_grad.shape[0]):
        anchor = (section_index - tick_index) % section_count
        first_span = jnp.sum(
            jnp.where(jnp.arange(section_count, dtype=jnp.int32) == anchor, start_column, 0)
        )
        span_index = (first_span + (anchor + tick_index) // section_count) % 2
        weight = lax.dynamic_index_in_dim(weights[:, 0], span_index, 0, keepdims=False)
        widened = carried.astype(jnp.float32)
        normed = (widened * rms_scale(widened)).astype(jnp.bfloat16)
        split_heads = widened.reshape(tok_rows, head_count, head_dim)
        queries = (split_heads * rms_scale(split_heads)).astype(jnp.bfloat16)
        projected = jnp.dot(normed, weight, preferred_element_type=jnp.float32)
        key_raw = projected[:, :head_dim]
        key_scale = rms_scale(key_raw)
        key_unit = key_raw * key_scale
        own_rows = jnp.concatenate([key_unit, projected[:, head_dim:]], axis=1).astype(jnp.bfloat16)
        gathered = lax.all_gather(own_rows, "ctx", axis=0, tiled=True)
        key_rows = gathered[:, :head_dim]
        value_rows = gathered[:, head_dim:]
        query_groups = queries.reshape(tok_rows, group_count, group_size, head_dim).transpose(
            1, 0, 2, 3
        )

        def forward_group(query_part):
            scores = (
                jnp.einsum("qhd,kd->hqk", query_part, key_rows, preferred_element_type=jnp.float32)
                * score_scale
            )
            exponent = jnp.where(causal[None], jnp.exp(scores), 0.0)
            total_weight = jnp.sum(exponent, axis=-1, keepdims=True)
            probs = (exponent / total_weight).astype(jnp.bfloat16)
            attended = jnp.einsum(
                "hqk,kd->qhd", probs, value_rows, preferred_element_type=jnp.float32
            )
            return (probs, attended)

        probs, attended = lax.map(forward_group, query_groups)
        output = attended.transpose(1, 0, 2, 3).reshape(tok_rows, feat_width)
        updated = (widened + output * rms_scale(output)).astype(jnp.bfloat16)
        carried = from_behind(updated, "pipe", 1)
        upstream = out_grad[tick_index, 0, 0]
        upstream_groups = upstream.reshape(tok_rows, group_count, group_size, head_dim).transpose(
            1, 0, 2, 3
        )
        row_delta = jnp.sum(upstream_groups.astype(jnp.float32) * attended, axis=-1).transpose(
            0, 2, 1
        )
        key_grad = jnp.zeros((tok_rows * lax.axis_size("ctx"), head_dim), jnp.float32)
        value_grad = jnp.zeros((tok_rows * lax.axis_size("ctx"), head_dim), jnp.float32)
        for head_block in range(group_count):
            prob_part = probs[head_block]
            value_grad = value_grad + jnp.einsum(
                "hqk,qhd->kd",
                prob_part,
                upstream_groups[head_block],
                preferred_element_type=jnp.float32,
            )
            prob_grad = jnp.einsum(
                "qhd,kd->hqk",
                upstream_groups[head_block],
                value_rows,
                preferred_element_type=jnp.float32,
            )
            score_grad = (
                prob_part.astype(jnp.float32)
                * (prob_grad - row_delta[head_block][..., None])
                * score_scale
            ).astype(jnp.bfloat16)
            key_grad = key_grad + jnp.einsum(
                "hqk,qhd->kd",
                score_grad,
                query_groups[head_block],
                preferred_element_type=jnp.float32,
            )
        key_sums = lax.psum_scatter(
            jnp.concatenate([key_grad, value_grad], axis=1).astype(jnp.bfloat16),
            "ctx",
            scatter_dimension=0,
            tiled=True,
        ).astype(jnp.float32)
        key_delta = key_sums[:, :head_dim]
        key_back = key_scale * (
            key_delta - key_unit * jnp.mean(key_delta * key_unit, axis=-1, keepdims=True)
        )
        grad_rows = jnp.concatenate([key_back, key_sums[:, head_dim:]], axis=1).astype(jnp.bfloat16)
        local_grad = lax.dot_general(
            normed, grad_rows, (((0,), (0,)), ((), ())), preferred_element_type=jnp.float32
        )
        span_mask = (jnp.arange(span_count, dtype=jnp.int32) == span_index).astype(jnp.float32)[
            :, None, None
        ]
        masked_grad = span_mask * local_grad
        weight_grads = weight_grads + masked_grad
    weight_grads = lax.psum(weight_grads, ("ctx", "dp"))
    return (carried[None, None], weight_grads[:, None])


def solution(mesh):
    return jax.shard_map(
        shards,
        mesh=mesh,
        in_specs=(
            P("pipe", "dp", "ctx", None),
            P(None, "pipe", None, None),
            P(None, "pipe", "dp", "ctx", None),
            P(None, "dp"),
            P(),
        ),
        out_specs=(P("pipe", "dp", "ctx", None), P(None, "pipe", None, None)),
        check_vma=False,
    )
```

profile of v0, /device:TPU:16, one launch (start us, length us, event | category | flops | bytes accessed | tf_op | source)
XLA Modules:
  0.0 990.2 jit_solution(8186478735265335391)
XLA Ops:
  16.2 74.4 %all-gather.3.cloned.1.call-done = bf16[2048,256]{1,0:T(8,128)(2,1)} async-done(((bf16[128,256]{1,0:T(8,128)(2,1)}), bf16[2048,256]{1,0:T(8,128)(2,1)}) %all-gather.3.cloned.1.call-update) | async-done | bytes 1048592 | tf_op jit(solution)/shard_map/all_gather | solution.py:65
  92.7 2.5 broadcast.232.clone2
  95.2 22.0 %while.26 = (s32[]{:T(128)}, bf16[2,4,128,2048]{2,3,1,0:T(8,128)(2,1)}, f32[2,128,4,128]{3,1,2,0:T(8,128)}, bf16[2,128,4,128]{1,3,2,0:T(8,128)(2,1)}, bf16[2048,...) while((s32[]{:T(128)}, ...), condition=%wide.region_7.8_spmd.clone, body=%wide.region_5.7_spmd.clone.sunk | while | flops 548666880 | bytes 33962720 | solution.py:85
  95.4 2.3 bitcast_reduce_fusion.4
  100.5 2.5 copy.225
  103.0 3.2 constant_dynamic-update-slice_fusion.4
  106.4 2.3 bitcast_reduce_fusion.4
  111.5 2.5 copy.225
  114.0 3.1 constant_dynamic-update-slice_fusion.4
  122.8 6.8 collective-permute-done
  134.4 2.3 convolution_bitcast_fusion.6
  136.7 2.3 fusion.38
  139.0 4.0 convolution_bitcast_fusion.8
  143.1 3.4 fusion.39
  149.1 56.5 %all-gather.5.cloned.1.call-done = bf16[2048,256]{1,0:T(8,128)(2,1)} async-done(((bf16[128,256]{1,0:T(8,128)(2,1)}), bf16[2048,256]{1,0:T(8,128)(2,1)}) %all-gather.5.cloned.1.call-update) | async-done | bytes 1048592 | tf_op jit(solution)/shard_map/all_gather | solution.py:65
  207.7 2.5 broadcast.232.clone
  210.1 22.0 %while.27 = (s32[]{:T(128)}, bf16[2,4,128,2048]{2,3,1,0:T(8,128)(2,1)}, f32[2,128,4,128]{3,1,2,0:T(8,128)}, bf16[2,128,4,128]{1,3,2,0:T(8,128)(2,1)}, bf16[2048,...) while((s32[]{:T(128)}, ...), condition=%wide.region_15.16_spmd.clone, body=%wide.region_13.15_spmd.clone.sunk | while | flops 548666880 | bytes 33962720 | solution.py:85
  210.4 2.3 bitcast_reduce_fusion.5
  215.5 2.5 copy.226
  218.0 3.2 constant_dynamic-update-slice_fusion.5
  221.4 2.3 bitcast_reduce_fusion.5
  226.5 2.5 copy.226
  229.0 3.1 constant_dynamic-update-slice_fusion.5
  233.6 2.3 convolution_bitcast_fusion.2
  235.9 2.3 fusion.36
  238.2 3.9 convolution_bitcast_fusion.4
  242.1 4.0 fusion.37
  248.4 35.8 %reduce-scatter.3.cloned.1.call-done = bf16[128,256]{1,0:T(8,128)(2,1)} async-done(((bf16[2048,256]{1,0:T(8,128)(2,1)}), bf16[128,256]{1,0:T(8,128)(2,1)}) %reduce-scatter.3.cloned.1.call-update) | async-done | bytes 65552 | tf_op jit(solution)/shard_map/reduce_scatter | solution.py:123
  287.2 73.8 %reduce-scatter.5.cloned.1.call-done = bf16[128,256]{1,0:T(8,128)(2,1)} async-done(((bf16[2048,256]{1,0:T(8,128)(2,1)}), bf16[128,256]{1,0:T(8,128)(2,1)}) %reduce-scatter.5.cloned.1.call-update) | async-done | bytes 65552 | tf_op jit(solution)/shard_map/reduce_scatter | solution.py:123
  370.5 7.2 collective-permute-done.1
  377.7 602.2 %all-reduce.2.cloned.1.call-done = f32[2,1,1024,256]{3,2,1,0:T(8,128)} async-done(((f32[2,1,1024,256]{3,2,1,0:T(8,128)}), f32[2,1,1024,256]{3,2,1,0:T(8,128)}) %all-reduce.2.cloned.1.call-update) | async-done | bytes 2097168 | tf_op jit(solution)/shard_map/psum | solution.py:142
  980.6 3.0 copy.256
  (160 shorter events, 53.3 us)
Async XLA Ops:
  7.2 3.3 copy-start
  7.2 8.0 copy-start.23
  7.2 83.4 %all-gather.3.cloned.1.call-start = ((), (), s32[]{:S(2)}) async-start(), calls=%async_computation.2 | async-start | bytes 1114112 | tf_op jit(solution)/shard_map/all_gather | solution.py:65
  12.6 192.9 %all-gather.5.cloned.1.call-start = ((), (), s32[]{:S(2)}) async-start(), calls=%async_computation.3 | async-start | bytes 1114112 | tf_op jit(solution)/shard_map/all_gather | solution.py:65
  95.2 24.8 %copy-start.1 = (bf16[1,1,128,1024]{3,2,1,0:T(8,128)(2,1)S(1)}, bf16[1,1,128,1024]{3,2,1,0:T(8,128)(2,1)}, u32[]{:S(2)}) copy-start(bf16[1,1,128,1024]{3,2,1,0:T(8,128)(2,1)} %param.9) | copy-start | bytes 786436
  95.2 2.6 copy-start.15
  103.0 3.2 copy-start.14
  103.0 3.2 copy-start.16
  106.2 2.6 copy-start.15
  114.0 3.1 copy-start.14
  114.0 3.1 copy-start.16
  117.1 14.0 %copy-start.8 = (bf16[2,1,1,128,1024]{4,3,2,1,0:T(8,128)(2,1)S(1)}, bf16[2,1,1,128,1024]{4,3,2,1,0:T(8,128)(2,1)}, u32[]{:S(2)}) copy-start(bf16[2,1,1,128,1024]{4,3,2,1,0:T(8,128)(2,1)} %param.11) | copy-start | bytes 1572868
  120.1 9.4 collective-permute-start
  129.6 18.6 %copy-start.2 = (bf16[128,1024]{1,0:T(8,128)(2,1)}, bf16[128,1024]{1,0:T(8,128)(2,1)S(1)}, u32[]{:S(2)}) copy-start(bf16[128,1024]{1,0:T(8,128)(2,1)S(1)} %collective-permute-done) | copy-start | bytes 786436
  130.0 4.4 copy-start.5
  131.1 153.1 %reduce-scatter.3.cloned.1.call-start = ((), (), s32[]{:S(2)}) async-start(), calls=%async_computation.4 | async-start | bytes 1114112 | tf_op jit(solution)/shard_map/reduce_scatter | solution.py:123
  147.6 213.4 %reduce-scatter.5.cloned.1.call-start = ((), (), s32[]{:S(2)}) async-start(), calls=%async_computation.5 | async-start | bytes 1114112 | tf_op jit(solution)/shard_map/reduce_scatter | solution.py:123
  210.1 2.6 copy-start.11
  218.0 3.2 copy-start.10
  218.0 3.2 copy-start.12
  221.2 2.6 copy-start.11
  229.0 3.1 copy-start.10
  229.0 3.1 copy-start.12
  232.1 3.8 copy-start.4
  232.1 6.1 copy-start.7
  242.1 44.6 %copy-start.20 = (f32[128]{0:T(128)S(1)}, f32[128]{0:T(128)}, u32[]{:S(2)}) copy-start(f32[128]{0:T(128)} %copy-done.19) | copy-start | bytes 1540
  246.1 114.8 %copy-start.6 = (f32[128,256]{1,0:T(8,128)S(1)}, f32[128,256]{1,0:T(8,128)}, u32[]{:S(2)}) copy-start(f32[128,256]{1,0:T(8,128)} %copy-done.5) | copy-start | bytes 393220
  246.1 114.8 %copy-start.18 = (f32[128]{0:T(128)S(1)}, f32[128]{0:T(128)}, u32[]{:S(2)}) copy-start(f32[128]{0:T(128)} %copy-done.17) | copy-start | bytes 1540
  246.1 117.4 %copy-start.3 = (bf16[128,1024]{1,0:T(8,128)(2,1)S(1)}, bf16[128,1024]{1,0:T(8,128)(2,1)}, u32[]{:S(2)}) copy-start(bf16[128,1024]{1,0:T(8,128)(2,1)} %copy-done.2) | copy-start | bytes 786436
  246.1 117.4 %copy-start.22 = (f32[128]{0:T(128)S(1)}, f32[128]{0:T(128)}, u32[]{:S(2)}) copy-start(f32[128]{0:T(128)} %copy-done.21) | copy-start | bytes 1540
  248.4 731.6 %all-reduce.2.cloned.1.call-start = ((), (), s32[]{:S(2)}) async-start(), calls=%async_computation.6 | async-start | bytes 4194304 | tf_op jit(solution)/shard_map/psum | solution.py:142
  368.5 9.2 collective-permute-start.1
  (7 other events, 13.1 us)
Sparse Core Ops, SparseCore 0:
  12.8 77.7 all-gather.2
  131.2 74.3 all-gather.4
  208.4 75.7 reduce-scatter.2
  287.7 73.2 reduce-scatter.4
  365.7 614.1 all-reduce.1
where the time goes:
time: 992 us; the launch traced here: 990 us
  waiting for transfers between devices  857 us (86%)
  local copies, waits for them, and re-layouts  44.1 us (4%)
  matrix products  43.5 us (4%)
  other arithmetic  25.8 us (3%)
  between operations  15.7 us (2%)
    psum x1, waiting for transfers between devices, shards(): weight_grads = lax.psum(weight_grads, ('ctx', 'dp'))  602 us
    all_gather x2, waiting for transfers between devices, shards(): gathered = lax.all_gather(own_rows, 'ctx', axis=0, tiled=True)  131 us
    reduce_scatter x2, waiting for transfers between devices, shards(): lax.psum_scatter(jnp.concatenate([key_grad, value_grad], axis=1).astype(j...  110 us
    dynamic_update_slice x8, local copies, waits for them, and re-layouts, shards(): probs, attended = lax.map(forward_group, query_groups)  22.5 us
  transfers between devices with their start and end apart: 7, of which 7 were waited for; matrix products, arithmetic and copies ran while one was open for 7% of the time, Pallas kernels for 0%

commit v1 on v0

--- a/solution.py
+++ b/solution.py
@@ -62,7 +62,9 @@
         key_scale = rms_scale(key_raw)
         key_unit = key_raw * key_scale
         own_rows = jnp.concatenate([key_unit, projected[:, head_dim:]], axis=1).astype(jnp.bfloat16)
-        gathered = lax.all_gather(own_rows, "ctx", axis=0, tiled=True)
+        gathered = jnp.concatenate(
+            lax.all_to_all(jnp.stack([own_rows] * lax.axis_size("ctx")), "ctx", 0, 0), axis=0
+        )
         key_rows = gathered[:, :head_dim]
         value_rows = gathered[:, head_dim:]
         query_groups = queries.reshape(tok_rows, group_count, group_size, head_dim).transpose(

time: 992 us -> 899 us (0.906)
  waiting for transfers between devices: 857 us -> 743 us
  starting transfers between devices: 4.23 us -> 22.3 us
    all_gather x2 -> x0, waiting for transfers between devices: 131 us -> none  [shards(): gathered = lax.all_gather(own_rows, 'ctx', axis=0, tiled=True)]
    all_to_all x0 -> x2, waiting for transfers between devices: none -> 32.1 us  [shards(): lax.all_to_all(jnp.stack([own_rows] * lax.axis_size('ctx')), 'ctx', 0, 0)]
    all_to_all x0 -> x2, starting transfers between devices: none -> 18.2 us  [shards(): lax.all_to_all(jnp.stack([own_rows] * lax.axis_size('ctx')), 'ctx', 0, 0)]
    reduce_scatter x2, waiting for transfers between devices: 110 us -> 99 us  [shards(): lax.psum_scatter(jnp.concatenate([key_grad, value_grad], axis=1).astype(j...]
  transfers between devices with their start and end apart: 7 -> 7, of which waited for: 7 -> 7; matrix products, arithmetic and copies ran while one was open for 7% -> 8% of each run, Pallas kernels for 0% -> 0%
where the time goes in v1:
time: 899 us; the launch traced here: 898 us
  waiting for transfers between devices  743 us (83%)
  local copies, waits for them, and re-layouts  49.8 us (6%)
  matrix products  43.5 us (5%)
  other arithmetic  23.6 us (3%)
  starting transfers between devices  22.3 us (2%)
  between operations  15.7 us (2%)
    psum x1, waiting for transfers between devices, shards(): weight_grads = lax.psum(weight_grads, ('ctx', 'dp'))  602 us
    reduce_scatter x2, waiting for transfers between devices, shards(): lax.psum_scatter(jnp.concatenate([key_grad, value_grad], axis=1).astype(j...  99 us
    all_to_all x2, waiting for transfers between devices, shards(): lax.all_to_all(jnp.stack([own_rows] * lax.axis_size('ctx')), 'ctx', 0, 0)  32.1 us
    dynamic_update_slice x8, local copies, waits for them, and re-layouts, shards(): probs, attended = lax.map(forward_group, query_groups)  22.6 us
    all_to_all x2, starting transfers between devices, shards(): lax.all_to_all(jnp.stack([own_rows] * lax.axis_size('ctx')), 'ctx', 0, 0)  18.2 us
  transfers between devices with their start and end apart: 7, of which 7 were waited for; matrix products, arithmetic and copies ran while one was open for 8% of the time, Pallas kernels for 0%

profile of v1, /device:TPU:16, one launch (start us, length us, event | category | flops | bytes accessed | tf_op | source)
XLA Modules:
  0.0 897.8 jit_solution(17873652809544849672)
XLA Ops:
  13.6 11.6 %all-to-all-start = ((bf16[16,128,256]{2,1,0:T(8,128)(2,1)}), bf16[16,128,256]{2,1,0:T(8,128)(2,1)S(1)}, u32[]{:S(2)}, u32[]{:S(2)}) async-start(bf16[16,128,256]{2,1,0:T(8,128)(2,1)} %stack.4), calls=%async_computation | async-start | bytes 2097152 | tf_op jit(solution)/shard_map/all_to_all | solution.py:66
  33.6 19.2 %all-to-all-done = bf16[16,128,256]{2,1,0:T(8,128)(2,1)S(1)} async-done(((bf16[16,128,256]{2,1,0:T(8,128)(2,1)}), bf16[16,128,256]{2,1,0:T(8,128)(2,1)S(1)}, u32[]{:S(2)}, u32[]{:S(2)}) %all-to-all-start) | async-done | bytes 1048608 | tf_op jit(solution)/shard_map/all_to_all | solution.py:66
  53.9 2.5 broadcast.234.clone2
  56.4 22.0 %while.26 = (s32[]{:T(128)}, bf16[2,4,128,2048]{2,3,1,0:T(8,128)(2,1)}, f32[2,128,4,128]{3,1,2,0:T(8,128)}, bf16[2,128,4,128]{1,3,2,0:T(8,128)(2,1)}, bf16[2048,...) while((s32[]{:T(128)}, ...), condition=%wide.region_7.8_spmd.clone, body=%wide.region_5.7_spmd.clone.sunk | while | flops 548666880 | bytes 33962720 | solution.py:87
  56.6 2.3 bitcast_reduce_fusion.4
  61.7 2.5 copy.225
  64.2 3.2 constant_dynamic-update-slice_fusion.4
  67.6 2.3 bitcast_reduce_fusion.4
  72.7 2.5 copy.225
  75.2 3.1 constant_dynamic-update-slice_fusion.4
  84.6 3.3 convolution_bitcast_fusion.6
  92.7 6.6 all-to-all-start.1
  100.1 3.3 fusion.38
  103.5 4.0 convolution_bitcast_fusion.8
  107.5 4.0 fusion.39
  111.5 2.3 pad_maximum_fusion
  114.5 12.9 %all-to-all-done.1 = bf16[16,128,256]{2,1,0:T(8,128)(2,1)} async-done(((bf16[16,128,256]{2,1,0:T(8,128)(2,1)}), bf16[16,128,256]{2,1,0:T(8,128)(2,1)}, u32[]{:S(2)}, u32[]{:S(2)}) %all-to-all-start.1) | async-done | bytes 1048608 | tf_op jit(solution)/shard_map/all_to_all | solution.py:66
  129.5 2.5 broadcast.234.clone
  132.0 19.9 %while.27 = (s32[]{:T(128)}, bf16[2,4,128,2048]{2,3,1,0:T(8,128)(2,1)}, f32[2,128,4,128]{3,1,2,0:T(8,128)}, bf16[2,128,4,128]{1,3,2,0:T(8,128)(2,1)S(1)}, bf16[2...) while((s32[]{:T(128)}, ...), condition=%wide.region_15.16_spmd.clone, body=%wide.region_13.15_spmd.clone.sunk | while | flops 548666880 | bytes 36059928 | solution.py:87
  136.2 2.5 copy.226
  138.7 3.2 constant_dynamic-update-slice_fusion.5
  146.2 2.5 copy.226
  148.7 3.1 constant_dynamic-update-slice_fusion.5
  153.4 2.3 convolution_bitcast_fusion.2
  155.7 2.3 fusion.36
  158.0 4.1 convolution_bitcast_fusion.4
  162.2 3.3 fusion.37
  166.7 25.3 %reduce-scatter.3.cloned.1.call-done = bf16[128,256]{1,0:T(8,128)(2,1)} async-done(((bf16[2048,256]{1,0:T(8,128)(2,1)}), bf16[128,256]{1,0:T(8,128)(2,1)}) %reduce-scatter.3.cloned.1.call-update) | async-done | bytes 65552 | tf_op jit(solution)/shard_map/reduce_scatter | solution.py:125
  194.9 73.7 %reduce-scatter.5.cloned.1.call-done = bf16[128,256]{1,0:T(8,128)(2,1)} async-done(((bf16[2048,256]{1,0:T(8,128)(2,1)}), bf16[128,256]{1,0:T(8,128)(2,1)}) %reduce-scatter.5.cloned.1.call-update) | async-done | bytes 65552 | tf_op jit(solution)/shard_map/reduce_scatter | solution.py:125
  278.2 7.5 collective-permute-done.1
  285.6 601.9 %all-reduce.2.cloned.1.call-done = f32[2,1,1024,256]{3,2,1,0:T(8,128)} async-done(((f32[2,1,1024,256]{3,2,1,0:T(8,128)}), f32[2,1,1024,256]{3,2,1,0:T(8,128)}) %all-reduce.2.cloned.1.call-update) | async-done | bytes 2097168 | tf_op jit(solution)/shard_map/psum | solution.py:144
  888.2 3.0 copy.256
  (180 shorter events, 59.0 us)
Async XLA Ops:
  7.2 3.2 copy-start
  7.2 18.6 %copy-start.1 = (bf16[1,1,128,1024]{3,2,1,0:T(8,128)(2,1)S(1)}, bf16[1,1,128,1024]{3,2,1,0:T(8,128)(2,1)}, u32[]{:S(2)}) copy-start(bf16[1,1,128,1024]{3,2,1,0:T(8,128)(2,1)} %param.9) | copy-start | bytes 786436
  10.4 3.2 copy-start.26
  13.5 19.1 %copy-start.31 = (s32[32]{0:T(128)S(1)}, s32[32]{0:T(128)}, u32[]{:S(2)}) copy-start(s32[32]{0:T(128)} %param.13) | copy-start | bytes 388
  13.6 39.3 %all-to-all-start = ((bf16[16,128,256]{2,1,0:T(8,128)(2,1)}), bf16[16,128,256]{2,1,0:T(8,128)(2,1)S(1)}, u32[]{:S(2)}, u32[]{:S(2)}) async-start(bf16[16,128,256]{2,1,0:T(8,128)(2,1)} %stack.4), calls=%async_computation | async-start | bytes 2097152 | tf_op jit(solution)/shard_map/all_to_all | solution.py:66
  52.9 3.5 copy-start.4
  64.2 3.2 copy-start.15
  64.2 3.2 copy-start.17
  78.3 6.2 copy-start.7
  81.3 8.7 collective-permute-start
  90.0 24.3 %copy-start.2 = (bf16[128,1024]{1,0:T(8,128)(2,1)}, bf16[128,1024]{1,0:T(8,128)(2,1)S(1)}, u32[]{:S(2)}) copy-start(bf16[128,1024]{1,0:T(8,128)(2,1)S(1)} %collective-permute-done) | copy-start | bytes 786436
  90.1 13.4 %copy-start.5 = (bf16[16,128,256]{2,1,0:T(8,128)(2,1)S(1)}, bf16[16,128,256]{2,1,0:T(8,128)(2,1)}, u32[]{:S(2)}) copy-start(bf16[16,128,256]{2,1,0:T(8,128)(2,1)} %copy-done.4) | copy-start | bytes 3145732
  92.7 34.7 %all-to-all-start.1 = ((bf16[16,128,256]{2,1,0:T(8,128)(2,1)}), bf16[16,128,256]{2,1,0:T(8,128)(2,1)}, u32[]{:S(2)}, u32[]{:S(2)}) async-start(bf16[16,128,256]{2,1,0:T(8,128)(2,1)} %stack.5), calls=%async_computation.1 | async-start | bytes 2097152 | tf_op jit(solution)/shard_map/all_to_all | solution.py:66
  99.3 92.6 %reduce-scatter.3.cloned.1.call-start = ((), (), s32[]{:S(2)}) async-start(), calls=%async_computation.4 | async-start | bytes 1114112 | tf_op jit(solution)/shard_map/reduce_scatter | solution.py:125
  103.5 4.0 copy-start.30
  113.8 154.8 %reduce-scatter.5.cloned.1.call-start = ((), (), s32[]{:S(2)}) async-start(), calls=%async_computation.5 | async-start | bytes 1114112 | tf_op jit(solution)/shard_map/reduce_scatter | solution.py:125
  138.7 3.2 copy-start.11
  138.7 3.2 copy-start.13
  138.7 3.2 copy-start.19
  148.7 3.1 copy-start.11
  148.7 3.1 copy-start.13
  148.7 3.1 copy-start.19
  151.9 3.8 copy-start.6
  153.4 4.7 copy-start.21
  162.1 30.5 %copy-start.23 = (f32[128]{0:T(128)S(1)}, f32[128]{0:T(128)}, u32[]{:S(2)}) copy-start(f32[128]{0:T(128)} %copy-done.22) | copy-start | bytes 1540
  162.1 32.3 %copy-start.27 = (f32[128]{0:T(128)S(1)}, f32[128]{0:T(128)}, u32[]{:S(2)}) copy-start(f32[128]{0:T(128)} %copy-done.26) | copy-start | bytes 1540
  165.5 103.2 %copy-start.9 = (f32[128,256]{1,0:T(8,128)S(1)}, f32[128,256]{1,0:T(8,128)}, u32[]{:S(2)}) copy-start(f32[128,256]{1,0:T(8,128)} %copy-done.8) | copy-start | bytes 393220
  165.5 103.2 %copy-start.25 = (f32[128]{0:T(128)S(1)}, f32[128]{0:T(128)}, u32[]{:S(2)}) copy-start(f32[128]{0:T(128)} %copy-done.24) | copy-start | bytes 1540
  165.5 105.7 %copy-start.3 = (bf16[128,1024]{1,0:T(8,128)(2,1)S(1)}, bf16[128,1024]{1,0:T(8,128)(2,1)}, u32[]{:S(2)}) copy-start(bf16[128,1024]{1,0:T(8,128)(2,1)} %copy-done.2) | copy-start | bytes 786436
  165.5 105.7 %copy-start.29 = (f32[128]{0:T(128)S(1)}, f32[128]{0:T(128)}, u32[]{:S(2)}) copy-start(f32[128]{0:T(128)} %copy-done.28) | copy-start | bytes 1540
  166.6 720.9 %all-reduce.2.cloned.1.call-start = ((), (), s32[]{:S(2)}) async-start(), calls=%async_computation.6 | async-start | bytes 4194304 | tf_op jit(solution)/shard_map/psum | solution.py:144
  276.2 9.4 %collective-permute-start.1 = (bf16[128,1024]{1,0:T(8,128)(2,1)S(1)}, bf16[128,1024]{1,0:T(8,128)(2,1)S(1)}, u32[]{:S(2)}, u32[]{:S(2)}) collective-permute-start(bf16[128,1024]{1,0:T(8,128)(2,1)S(1)} %add_convert_fusion), channel_id=1, source_target_pairs={{448,0},{0,64},{64,128},{128,192},{192,256},{256,320},{320,384},{3... | collective-permute-start | bytes 786440 | tf_op jit(solution)/shard_map/ppermute | solution.py:13
  (17 other events, 29.3 us)
Sparse Core Ops, SparseCore 0:
  114.0 77.9 reduce-scatter.2
  195.5 73.0 reduce-scatter.4
  273.4 614.0 all-reduce.1
